TPU v7x, 32 devices: a whole 2x2x4 slice. The times are simulated.
32 devices in a mesh: groups: 2 (over x), utt: 16 (over z, y, core).
Axes of the slice: x: 2, y: 2, z: 4, core: 2. Of those that a mesh axis runs over, the one named last changes fastest.
Arguments:
- cache_kv: bfloat16 [512, 8, 3072], P(('groups', 'utt')), parts along dimension 0, may hold values from -160 to 160
- new_rows: bfloat16 [512, 4608], P(('groups', 'utt')), parts along dimension 0, may hold values from -6 to 6
- cross_queries: bfloat16 [512, 1536], P(('groups', 'utt')), parts along dimension 0, may hold values from -6 to 6
- enc_kv: bfloat16 [32, 256, 3072], P(('groups', 'utt')), parts along dimension 0, may hold values from -160 to 160
- lengths: int32 [32], P(('groups', 'utt')), parts along dimension 0, may hold values from 64 to 256, as said below
- parents: int32 [32, 16], P(('groups', 'utt')), parts along dimension 0, may hold values from 0 to 15
Outputs:
- mixed: bfloat16 [512, 1536], P(('groups', 'utt')), parts along dimension 0
There are 2 independent parts, one for each index of `groups`. A program takes and returns all parts, laid end to end along the dimension named above; each array names one. Nothing has to cross between parts.
Inputs may be any that keep to these rules, and one draw needn't show every extreme that they name: `lengths`: some utterance of each part has all 256 frames.
All inputs are finite; a program needn't handle non-finite values.
Results may differ from a plain program's by a relative error of at most 0.009.
Values may be sent and summed in bfloat16 or wider, within the bound.
A program may use at most 64 MiB of HBM per device.

v0:
```python
import jax
import jax.numpy as jnp
from jax import lax
from jax.sharding import PartitionSpec as P

HD = 128


def reorder(cache_rows, parents):
    utterances, beam_width = parents.shape
    grouped = cache_rows.reshape(utterances, beam_width, cache_rows.shape[1], cache_rows.shape[2])
    picked = jax.vmap(lambda block, picks: block[picks])(grouped, parents)
    return picked.reshape(cache_rows.shape)


def attend_self(query, old_keys, old_values, new_key, new_value):
    row_count = query.shape[0]
    history = old_keys.shape[1]
    head_count = query.shape[1] // HD
    scale = HD ** (-0.5)
    query_heads = query.reshape(row_count, head_count, HD)
    key_heads = old_keys.reshape(row_count, history, head_count, HD)
    value_heads = old_values.reshape(row_count, history, head_count, HD)
    old_scores = (
        jnp.einsum("rhd,rthd->rht", query_heads, key_heads, preferred_element_type=jnp.float32)
        * scale
    )
    own_score = (
        jnp.einsum(
            "rhd,rhd->rh",
            query_heads,
            new_key.reshape(row_count, head_count, HD),
            preferred_element_type=jnp.float32,
        )
        * scale
    )
    peak = jnp.maximum(jnp.max(old_scores, axis=2), own_score)
    old_exp = jnp.exp(old_scores - peak[:, :, None])
    own_exp = jnp.exp(own_score - peak)
    total = jnp.sum(old_exp, axis=2) + own_exp
    old_weight = (old_exp / total[:, :, None]).astype(jnp.bfloat16)
    own_weight = (own_exp / total).astype(jnp.bfloat16)
    context = jnp.einsum(
        "rht,rthd->rhd", old_weight, value_heads, preferred_element_type=jnp.float32
    )
    context = context + own_weight.astype(jnp.float32)[:, :, None] * new_value.reshape(
        row_count, head_count, HD
    ).astype(jnp.float32)
    return context.reshape(row_count, head_count * HD).astype(jnp.bfloat16)


def attend_frames(queries, frames_kv, frame_counts):
    utterances = frame_counts.shape[0]
    beam_width = queries.shape[0] // utterances
    feature = queries.shape[1]
    head_count = feature // HD
    frame_total = frames_kv.shape[1]
    scale = HD ** (-0.5)
    query_heads = queries.reshape(utterances, beam_width, head_count, HD)
    key_heads = frames_kv[:, :, :feature].reshape(utterances, frame_total, head_count, HD)
    value_heads = frames_kv[:, :, feature:].reshape(utterances, frame_total, head_count, HD)
    scores = (
        jnp.einsum("ubhd,ufhd->uhbf", query_heads, key_heads, preferred_element_type=jnp.float32)
        * scale
    )
    live = (
        lax.broadcasted_iota(jnp.int32, (utterances, 1, 1, frame_total), 3)
        < frame_counts[:, None, None, None]
    )
    scores = jnp.where(live, scores, -1e30)
    peak = jnp.max(scores, axis=3, keepdims=True)
    raised = jnp.where(live, jnp.exp(scores - peak), 0.0)
    weights = (raised / jnp.sum(raised, axis=3, keepdims=True)).astype(jnp.bfloat16)
    context = jnp.einsum(
        "uhbf,ufhd->ubhd", weights, value_heads, preferred_element_type=jnp.float32
    )
    return context.reshape(utterances * beam_width, feature)


def body(cache_kv, new_rows, cross_queries, enc_kv, lengths, parents):
    feature = cross_queries.shape[1]
    cross_context = attend_frames(cross_queries, enc_kv, lengths)
    arrived, new_here = (
        lax.all_to_all(cache_kv, "utt", split_axis=0, concat_axis=0, tiled=True),
        lax.all_to_all(new_rows, "utt", split_axis=0, concat_axis=0, tiled=True),
    )
    reordered = reorder(arrived, parents)
    self_context = attend_self(
        new_here[:, :feature],
        reordered[:, :, :feature],
        reordered[:, :, feature:],
        new_here[:, feature : 2 * feature],
        new_here[:, 2 * feature :],
    )
    mixed_here = (self_context.astype(jnp.float32) + cross_context).astype(jnp.bfloat16)
    mixed = lax.all_to_all(mixed_here, "utt", split_axis=0, concat_axis=0, tiled=True)
    return mixed


def solution(mesh):
    placed = (
        P(("groups", "utt"), None, None),
        P(("groups", "utt"), None),
        P(("groups", "utt"), None),
        P(("groups", "utt"), None, None),
        P(("groups", "utt")),
        P(("groups", "utt"), None),
    )
    return jax.shard_map(
        body, mesh=mesh, in_specs=placed, out_specs=P(("groups", "utt"), None), check_vma=False
    )
```

profile of v0, /device:TPU:0, one launch (start us, length us, event | category | flops | bytes accessed | tf_op | source)
XLA Modules:
  0.0 55.8 jit_solution(18194679548267514697)
XLA Ops:
  0.0 0.0 copy-start
  0.0 0.5 broadcast.47
  0.5 1.6 %reduce.6 = bf16[16,4608]{1,0:T(8,128)(2,1)S(1)} reduce(bf16[16,1,4608]{2,0,1:T(8,128)(2,1)} %bitcast.68, bf16[]{:T(256)} %broadcast.47), dimensions={1}, to_apply=%copy.29.reduce_sub_computation | reduce | bytes 294914 | tf_op jit(solution)/shard_map/all_to_all | solution.py:85
  2.1 0.7 %reshape.136 = bf16[16,2,2304]{2,1,0:T(2,128)(2,1)} reshape(bf16[16,4608]{1,0:T(8,128)(2,1)S(1)} %reduce.6) | data formatting | bytes 294912
  2.8 7.4 %all-to-all-start.1 = ((bf16[16,2,2304]{2,1,0:T(2,128)(2,1)}), bf16[16,2,2304]{2,1,0:T(2,128)(2,1)S(1)}, u32[]{:S(2)}, u32[]{:S(2)}) async-start(bf16[16,2,2304]{2,1,0:T(2,128)(2,1)} %reshape.136), calls=%async_computation.1 | async-start | bytes 294912 | tf_op jit(solution)/shard_map/all_to_all | solution.py:85
  10.2 1.5 %fusion.19 = (bf16[1,256,1536]{2,1,0:T(8,128)(2,1)S(1)}, bf16[1,256,1536]{2,1,0:T(8,128)(2,1)S(1)}) fusion(bf16[1,256,3072]{2,1,0:T(8,128)(2,1)} %param.9), kind=kLoop, calls=%fused_computation.41 | loop fusion | bytes 3145728 | tf_op jit(solution)/shard_map/slice | solution.py:60
  11.7 0.3 copy.51
  12.6 0.3 copy.52
  12.9 5.5 %all-to-all-done.1 = bf16[16,2,2304]{2,1,0:T(2,128)(2,1)S(1)} async-done(((bf16[16,2,2304]{2,1,0:T(2,128)(2,1)}), bf16[16,2,2304]{2,1,0:T(2,128)(2,1)S(1)}, u32[]{:S(2)}, u32[]{:S(2)}) %all-to-all-start.1) | async-done | bytes 147488 | tf_op jit(solution)/shard_map/all_to_all | solution.py:85
  18.4 3.6 %all-to-all-start = ((bf16[16,8,3072]{2,1,0:T(8,128)(2,1)}), bf16[16,8,3072]{2,1,0:T(8,128)(2,1)S(1)}, u32[]{:S(2)}, u32[]{:S(2)}) async-start(bf16[16,8,3072]{2,1,0:T(8,128)(2,1)} %param.6), calls=%async_computation | async-start | bytes 1572864 | tf_op jit(solution)/shard_map/all_to_all | solution.py:84
  22.0 0.0 copy-start.1
  22.0 0.0 copy-done
  22.0 0.4 fusion.21
  22.4 0.4 convolution_bitcast_fusion
  22.9 0.0 copy-done.1
  22.9 0.1 reshape.137
  23.1 0.1 reshape.110
  23.2 0.1 reshape.111
  23.2 0.1 fusion.8
  23.3 0.1 copy.43
  23.5 17.2 %all-to-all-done = bf16[16,8,3072]{2,1,0:T(8,128)(2,1)S(1)} async-done(((bf16[16,8,3072]{2,1,0:T(8,128)(2,1)}), bf16[16,8,3072]{2,1,0:T(8,128)(2,1)S(1)}, u32[]{:S(2)}, u32[]{:S(2)}) %all-to-all-start) | async-done | bytes 786464 | tf_op jit(solution)/shard_map/all_to_all | solution.py:84
  40.7 0.6 %gather_fusion = bf16[16,8,3072]{2,1,0:T(8,128)(2,1)S(1)} fusion(bf16[1,16,8,3072]{3,2,1,0:T(8,128)(2,1)S(1)} %bitcast.64, s32[16]{0:T(128)S(1)} %or_bitcast_fusion), kind=kCustom, calls=%fused_computation | custom fusion | bytes 1572992 | tf_op jit(solution)/shard_map/vmap()/gather | solution.py:12
  41.3 0.3 fusion.5
  41.6 0.1 copy.39
  41.8 0.1 copy.44
  42.0 0.3 fusion.6
  42.3 0.1 copy.30
  42.4 0.1 fusion.10
  42.6 0.7 %reduce.7 = bf16[16,1536]{1,0:T(8,128)(2,1)S(1)} reduce(bf16[16,1,1536]{2,0,1:T(8,128)(2,1)S(1)} %add_convert_fusion, bf16[]{:T(256)} %broadcast.47), dimensions={1}, to_apply=%copy.37.reduce_sub_computation | reduce | bytes 98306 | tf_op jit(solution)/shard_map/convert_element_type | solution.py:95
  43.2 11.9 %all_to_all.26 = bf16[16,2,768]{2,1,0:T(2,128)(2,1)S(1)} all-to-all(bf16[16,2,768]{2,1,0:T(2,128)(2,1)S(1)} %reshape.138), channel_id=1, replica_groups=mesh['groups'=2,'utt'=16] {'utt'}, dimensions={0} | all-to-all | bytes 98304 | tf_op jit(solution)/shard_map/all_to_all | solution.py:96
  55.2 0.6 %copy.66 = bf16[16,1,1536]{2,0,1:T(8,128)(2,1)} copy(bf16[16,1,1536]{2,1,0:T(2,128)(2,1)S(1)} %reshape.139) | data formatting | bytes 98304
  (19 shorter events, 0.4 us)
Async XLA Ops:
  0.0 22.0 %copy-start = (bf16[16,1536]{1,0:T(8,128)(2,1)S(1)}, bf16[16,1536]{1,0:T(8,128)(2,1)}, u32[]{:S(2)}) copy-start(bf16[16,1536]{1,0:T(8,128)(2,1)} %param.8) | copy-start | bytes 147460
  2.8 15.6 %all-to-all-start.1 = ((bf16[16,2,2304]{2,1,0:T(2,128)(2,1)}), bf16[16,2,2304]{2,1,0:T(2,128)(2,1)S(1)}, u32[]{:S(2)}, u32[]{:S(2)}) async-start(bf16[16,2,2304]{2,1,0:T(2,128)(2,1)} %reshape.136), calls=%async_computation.1 | async-start | bytes 294912 | tf_op jit(solution)/shard_map/all_to_all | solution.py:85
  18.4 22.3 %all-to-all-start = ((bf16[16,8,3072]{2,1,0:T(8,128)(2,1)}), bf16[16,8,3072]{2,1,0:T(8,128)(2,1)S(1)}, u32[]{:S(2)}, u32[]{:S(2)}) async-start(bf16[16,8,3072]{2,1,0:T(8,128)(2,1)} %param.6), calls=%async_computation | async-start | bytes 1572864 | tf_op jit(solution)/shard_map/all_to_all | solution.py:84
  22.0 0.8 %copy-start.1 = (s32[1,16]{1,0:T(1,128)S(1)}, s32[1,16]{1,0:T(1,128)}, u32[]{:S(2)}) copy-start(s32[1,16]{1,0:T(1,128)} %param.11) | copy-start | bytes 196
where the time goes:
time: 56.2 us; the launch traced here: 55.8 us
  waiting for transfers between devices  22.7 us (40%)
  blocking collectives  11.9 us (21%)
  starting transfers between devices  11 us (20%)
  local copies, waits for them, and re-layouts  5.25 us (9%)
  other arithmetic  2.63 us (5%)
  matrix products  1.41 us (3%)
  between operations  0.92 us (2%)
    all_to_all x1, waiting for transfers between devices, body(): lax.all_to_all(cache_kv, 'utt', split_axis=0, concat_axis=0, tiled=True)  17.2 us
    all_to_all x1, blocking collectives, body(): lax.all_to_all(mixed_here, 'utt', split_axis=0, concat_axis=0, tiled=True)  11.9 us
    all_to_all x1, starting transfers between devices, body(): lax.all_to_all(new_rows, 'utt', split_axis=0, concat_axis=0, tiled=True)  7.41 us
    all_to_all x1, waiting for transfers between devices, body(): lax.all_to_all(new_rows, 'utt', split_axis=0, concat_axis=0, tiled=True)  5.47 us
    all_to_all x1, starting transfers between devices, body(): lax.all_to_all(cache_kv, 'utt', split_axis=0, concat_axis=0, tiled=True)  3.62 us
    unnamed x12, local copies, waits for them, and re-layouts  2.06 us
    all_to_all x1, other arithmetic, body(): lax.all_to_all(new_rows, 'utt', split_axis=0, concat_axis=0, tiled=True)  1.6 us
    slice x1, local copies, waits for them, and re-layouts, attend_frames(): frames_kv[:, :, :feature].reshape(utterances, frame_total, head_count, HD)  1.47 us
  transfers between devices with their start and end apart: 2, of which 2 were waited for; matrix products, arithmetic and copies ran while one was open for 6% of the time, Pallas kernels for 0%

commit v1 on v0

--- a/solution.py
+++ b/solution.py
@@ -1,9 +1,324 @@
+import functools
+
 import jax
 import jax.numpy as jnp
 from jax import lax
+from jax.experimental import pallas as pl
+from jax.experimental.pallas import tpu as pltpu
 from jax.sharding import PartitionSpec as P
 
 HD = 128
+CORES = 2
+LINES = 2
+PARTS = 3
+LOW = -1e30
+
+
+def contract_last(a, b):
+    return lax.dot_general(a, b, (((1,), (1,)), ((), ())), preferred_element_type=jnp.float32)
+
+
+def fast_kernel(
+    n,
+    cache_ref, new_ref, cq_ref, enc_ref, len_ref, par_ref,
+    out_ref,
+    qbuf, kbuf, vbuf, newbuf, cqbuf, encbuf, ptab, ctx, ybuf, sbuf, zbuf, xsend, xrecv,
+    local_sem, q_send, q_recv, f_send, c_send, c_recv, p_send, p_recv, x_send, x_recv,
+    y_send, y_recv, z_send, z_recv,
+):
+    feature = cq_ref.shape[1]
+    half = feature // CORES
+    heads = half // HD
+    rows = cq_ref.shape[0]
+    utts = new_ref.shape[0]
+    old = cache_ref.shape[0]
+    history = old // utts
+    depth = n // (CORES * LINES)
+    scale = HD ** (-0.5)
+
+    me = lax.axis_index("utt")
+    z = me // (CORES * LINES)
+    y = (me // CORES) % LINES
+    c = me % CORES
+    y_other = 1 - y
+    c_other = 1 - c
+
+    def at(zz, yy, cc):
+        return (zz * LINES + yy) * CORES + cc
+
+    def remote(src, dst, ssem, rsem, dev):
+        return pltpu.make_async_remote_copy(
+            src_ref=src, dst_ref=dst, send_sem=ssem, recv_sem=rsem,
+            device_id={"utt": dev}, device_id_type=pl.DeviceIdType.MESH,
+        )
+
+    barrier = pltpu.get_barrier_semaphore()
+    for k in range(1, n):
+        pl.semaphore_signal(
+            barrier, inc=1, device_id={"utt": lax.rem(me + k, n)},
+            device_id_type=pl.DeviceIdType.MESH,
+        )
+
+    my_half = pl.ds(pl.multiple_of(c * half, HD), half)
+    my_values = pl.ds(pl.multiple_of(feature + c * half, HD), half)
+    my_rows = pl.ds(pl.multiple_of(c * old, old), old)
+    copies = [
+        pltpu.make_async_copy(cq_ref, cqbuf, local_sem.at[0]),
+        pltpu.make_async_copy(enc_ref.at[0], encbuf, local_sem.at[1]),
+        pltpu.make_async_copy(new_ref, newbuf, local_sem.at[2]),
+        pltpu.make_async_copy(new_ref.at[:, my_half], qbuf.at[z, y, c], local_sem.at[3]),
+        pltpu.make_async_copy(cache_ref.at[:, my_half], kbuf.at[my_rows], local_sem.at[4]),
+        pltpu.make_async_copy(cache_ref.at[:, my_values], vbuf.at[my_rows], local_sem.at[5]),
+        pltpu.make_async_copy(par_ref, ptab.at[me], local_sem.at[6]),
+    ]
+    for cp in copies:
+        cp.start()
+
+    pl.semaphore_wait(barrier, n - 1)
+
+    sends = []
+    slot = 0
+    for dz in (2, 1, 3, 0):
+        zz = lax.rem(z + dz, depth)
+        for dc in range(CORES):
+            cc = lax.rem(c + dc, CORES)
+            cols = pl.ds(pl.multiple_of(cc * half, HD), half)
+            for yy in (y, y_other) if dz == 0 else (y,):
+                if dz == 0 and dc == 0 and yy is y:
+                    continue
+                cp = remote(new_ref.at[:, cols], qbuf.at[z, y, c], q_send.at[slot],
+                            q_recv.at[me], at(zz, yy, cc))
+                cp.start()
+                sends.append(cp)
+                slot += 1
+    for k in range(1, n):
+        dev = lax.rem(me + k, n)
+        cp = remote(par_ref, ptab.at[me], p_send.at[k - 1], p_recv.at[me], dev)
+        cp.start()
+        sends.append(cp)
+    other_half = pl.ds(pl.multiple_of(c_other * half, HD), half)
+    other_values = pl.ds(pl.multiple_of(feature + c_other * half, HD), half)
+    partner = at(z, y, c_other)
+    cache_in = []
+    for i, (cols, buf) in enumerate(((other_half, kbuf), (other_values, vbuf))):
+        cp = remote(cache_ref.at[:, cols], buf.at[my_rows], c_send.at[i], c_recv.at[i], partner)
+        cp.start()
+        sends.append(cp)
+        cache_in.append(cp)
+
+    copies[0].wait()
+    copies[1].wait()
+
+    frames = encbuf.shape[0]
+    live = lax.broadcasted_iota(jnp.int32, (rows, frames), 1) < len_ref[0]
+    ones_f = jnp.ones((frames, HD), jnp.bfloat16)
+
+    def cross(h):
+        cols = slice(h * HD, (h + 1) * HD)
+        s = contract_last(cqbuf[:, cols], encbuf[:, cols]) * scale
+        s = jnp.where(live, s, LOW)
+        p = jnp.where(live, jnp.exp(s - jnp.max(s, axis=1, keepdims=True)), 0.0).astype(jnp.bfloat16)
+        v = jnp.concatenate([encbuf[:, feature + h * HD : feature + (h + 1) * HD], ones_f], axis=1)
+        o = jnp.dot(p, v, preferred_element_type=jnp.float32)
+        o = o[:, :HD] / o[:, HD:]
+        for b in range(rows):
+            xsend[b, :, cols] = o[b : b + 1, :]
+
+    for h in range(feature // HD):
+        cross(h)
+
+    own_x = pltpu.make_async_copy(xsend.at[me], xrecv.at[me], local_sem.at[7])
+    own_x.start()
+    for k in range(1, n):
+        dev = lax.rem(me + k, n)
+        cp = remote(xsend.at[dev], xrecv.at[me], x_send.at[k - 1], x_recv.at[me], dev)
+        cp.start()
+        sends.append(cp)
+
+    copies[3].wait()
+    slot = 0
+    for dz in (1, 3, 2):
+        zz = lax.rem(z + dz, depth)
+        for cc in range(CORES):
+            src = at(zz, y, cc)
+            piece = qbuf.at[zz, y, cc]
+            remote(piece, piece, f_send.at[slot], q_recv.at[src], src).wait_recv()
+            cp = remote(piece, piece, f_send.at[slot], q_recv.at[src], at(z, y_other, c))
+            cp.start()
+            sends.append(cp)
+            slot += 1
+    piece = qbuf.at[z, y, c_other]
+    remote(piece, piece, f_send.at[0], q_recv.at[partner], partner).wait_recv()
+
+    copies[4].wait()
+    copies[5].wait()
+    for cp in cache_in:
+        cp.wait_recv()
+    copies[6].wait()
+    for k in range(1, n):
+        src = lax.rem(me + n - k, n)
+        remote(par_ref, ptab.at[src], p_send.at[0], p_recv.at[src], src).wait_recv()
+
+    table = jnp.concatenate([ptab[u] for u in range(utts)], axis=0)
+    beam_lane = lax.broadcasted_iota(jnp.int32, table.shape, 1)
+    row_u = lax.broadcasted_iota(jnp.int32, (utts, 1), 0)
+    chip = me // CORES
+    keys = CORES * old
+    ones_k = jnp.ones((keys, HD), jnp.bfloat16)
+
+    def partial(yy):
+        target = []
+        for zz in range(depth):
+            for cc in range(CORES):
+                col = jnp.sum(jnp.where(beam_lane == at(zz, yy, cc), table, 0), axis=1, keepdims=True)
+                target.append((col - chip * CORES) * utts + row_u)
+        target = jnp.concatenate(target, axis=0)
+        count = depth * CORES * utts
+        valid = lax.broadcasted_iota(jnp.int32, (count, keys), 1) // history == target
+        sel = jnp.broadcast_to((target >= 0) & (target < CORES * utts), (count, HD))
+        lane = lax.broadcasted_iota(jnp.int32, (count, HD), 1)
+        stats = jnp.zeros((count, HD), jnp.float32)
+        for h in range(heads):
+            cols = slice(h * HD, (h + 1) * HD)
+            q = qbuf[:, pl.ds(yy, 1), :, :, cols].reshape(count, HD)
+            s = jnp.where(valid, contract_last(q, kbuf[:, cols]) * scale, LOW)
+            m = jnp.max(s, axis=1, keepdims=True)
+            p = jnp.where(valid, jnp.exp(s - m), 0.0).astype(jnp.bfloat16)
+            v = jnp.concatenate([vbuf[:, cols], ones_k], axis=1)
+            o = jnp.dot(p, v, preferred_element_type=jnp.float32)
+            total = jnp.where(sel, o[:, HD:], 1.0)
+            ctx[:, pl.ds(yy, 1), :, :, cols] = (o[:, :HD] / total).astype(jnp.bfloat16).reshape(
+                depth, 1, CORES, utts, HD)
+            rest = jnp.where(sel, m + jnp.log(total), 0.0)
+            for k in range(PARTS):
+                part = rest.astype(jnp.bfloat16).astype(jnp.float32)
+                stats = jnp.where(lane == PARTS * h + k, part, stats)
+                rest = rest - part
+        ctx[:, pl.ds(yy, 1), :, :, half:] = stats.astype(jnp.bfloat16).reshape(
+            depth, 1, CORES, utts, HD)
+
+    partial(y)
+
+    for zz in range(depth):
+        for cc in range(CORES):
+            src = at(zz, y_other, cc)
+            piece = qbuf.at[zz, y_other, cc]
+            remote(piece, piece, f_send.at[0], q_recv.at[src], src).wait_recv()
+    partial(y_other)
+
+    across = at(z, y_other, c)
+    y_in = []
+    for dz in (2, 1, 3, 0):
+        zz = lax.rem(z + dz, depth)
+        cp = remote(ctx.at[zz, y_other], ybuf.at[dz], y_send.at[dz], y_recv.at[dz], across)
+        cp.start()
+        sends.append(cp)
+        y_in.append((dz, zz, cp))
+
+    copies[2].wait()
+    own = []
+    for h in range(feature // HD):
+        q = newbuf[:, h * HD : (h + 1) * HD].astype(jnp.float32)
+        k = newbuf[:, feature + h * HD : feature + (h + 1) * HD].astype(jnp.float32)
+        own.append(jnp.sum(q * k, axis=1, keepdims=True) * scale)
+
+    slot = 0
+    for dz, zz, cp in y_in:
+        cp.wait_recv()
+        sbuf[dz] = (ctx[pl.ds(zz, 1), pl.ds(y, 1)].reshape(CORES, utts, half + HD) + ybuf[dz])
+        for dc in range(CORES):
+            cc = lax.rem(c + dc, CORES)
+            if dz == 0 and dc == 0:
+                stay = pltpu.make_async_copy(sbuf.at[dz, cc], zbuf.at[z, c], local_sem.at[8])
+                stay.start()
+                continue
+            cp = remote(sbuf.at[dz, cc], zbuf.at[z, c], z_send.at[slot], z_recv.at[z * CORES + c],
+                        at(zz, y, cc))
+            cp.start()
+            sends.append(cp)
+            slot += 1
+
+    own_x.wait()
+    for k in range(1, n):
+        src = lax.rem(me + n - k, n)
+        remote(xsend.at[src], xrecv.at[src], x_send.at[0], x_recv.at[src], src).wait_recv()
+
+    stay.wait()
+    for dz in range(depth):
+        zz = lax.rem(z + dz, depth)
+        for dc in range(CORES):
+            if dz == 0 and dc == 0:
+                continue
+            cc = lax.rem(c + dc, CORES)
+            remote(zbuf.at[zz, cc], zbuf.at[zz, cc], z_send.at[0], z_recv.at[zz * CORES + cc],
+                   at(zz, y, cc)).wait_recv()
+
+    for cc in range(CORES):
+        both = zbuf[0, cc].astype(jnp.float32)
+        for zz in range(1, depth):
+            both = both + zbuf[zz, cc].astype(jnp.float32)
+        stats = both[:, half:]
+        lane = lax.broadcasted_iota(jnp.int32, stats.shape, 1)
+        for hl in range(heads):
+            h = cc * heads + hl
+            cols = slice(h * HD, (h + 1) * HD)
+            mine = (lane >= PARTS * hl) & (lane < PARTS * (hl + 1))
+            lse = jnp.sum(jnp.where(mine, stats, 0.0), axis=1, keepdims=True)
+            peak = jnp.maximum(lse, own[h])
+            w_old = jnp.exp(lse - peak)
+            w_own = jnp.exp(own[h] - peak)
+            inv = 1.0 / (w_old + w_own)
+            value = newbuf[:, 2 * feature + h * HD : 2 * feature + (h + 1) * HD].astype(jnp.float32)
+            self_ctx = both[:, hl * HD : (hl + 1) * HD] * (w_old * inv) + value * (w_own * inv)
+            crossed = jnp.concatenate([xrecv[u, :, cols] for u in range(utts)], axis=0)
+            out_ref[:, cols] = (
+                self_ctx.astype(jnp.bfloat16).astype(jnp.float32) + crossed
+            ).astype(jnp.bfloat16)
+
+    for cp in sends:
+        cp.wait_send()
+
+
+def fast_body(n, cache_kv, new_rows, cross_queries, enc_kv, lengths, parents):
+    rows, feature = cross_queries.shape
+    utts, history, width = cache_kv.shape
+    half = feature // CORES
+    old = utts * history
+    depth = n // (CORES * LINES)
+    frames = enc_kv.shape[1]
+    bf = jnp.bfloat16
+    dma = pltpu.SemaphoreType.DMA
+    hbm = pl.BlockSpec(memory_space=pl.ANY)
+    return pl.pallas_call(
+        functools.partial(fast_kernel, n),
+        out_shape=jax.ShapeDtypeStruct((utts, feature), bf),
+        in_specs=[hbm, hbm, hbm, hbm, pl.BlockSpec(memory_space=pltpu.SMEM),
+                  pl.BlockSpec(memory_space=pltpu.VMEM)],
+        out_specs=pl.BlockSpec(memory_space=pltpu.VMEM),
+        scratch_shapes=[
+            pltpu.VMEM((depth, LINES, CORES, utts, half), bf),
+            pltpu.VMEM((CORES * old, half), bf),
+            pltpu.VMEM((CORES * old, half), bf),
+            pltpu.VMEM(new_rows.shape, bf),
+            pltpu.VMEM(cross_queries.shape, bf),
+            pltpu.VMEM((frames, width), bf),
+            pltpu.VMEM((n,) + parents.shape, jnp.int32),
+            pltpu.VMEM((depth, LINES, CORES, utts, half + HD), bf),
+            pltpu.VMEM((depth, CORES, utts, half + HD), bf),
+            pltpu.VMEM((depth, CORES, utts, half + HD), bf),
+            pltpu.VMEM((depth, CORES, utts, half + HD), bf),
+            pltpu.VMEM((rows, 1, feature), jnp.float32),
+            pltpu.VMEM((utts, 1, feature), jnp.float32),
+            dma((9,)),
+            dma((depth * CORES + 1,)), dma((n,)), dma(((depth - 1) * CORES,)),
+            dma((2,)), dma((2,)),
+            dma((n - 1,)), dma((n,)), dma((n - 1,)), dma((n,)),
+            dma((depth,)), dma((depth,)), dma((depth * CORES - 1,)), dma((depth * CORES,)),
+        ],
+        compiler_params=pltpu.CompilerParams(
+            collective_id=0, has_side_effects=True, vmem_limit_bytes=48 << 20
+        ),
+    )(cache_kv.reshape(old, width), new_rows, cross_queries, enc_kv, lengths, parents)
 
 
 def reorder(cache_rows, parents):
@@ -106,6 +421,20 @@
         P(("groups", "utt")),
         P(("groups", "utt"), None),
     )
+    n = mesh.shape["utt"]
+
+    def either(cache_kv, new_rows, cross_queries, enc_kv, lengths, parents):
+        feature = cross_queries.shape[1]
+        fits = (
+            parents.shape == (1, n)
+            and cache_kv.shape[0] == n
+            and n == 4 * CORES * LINES
+            and feature % (CORES * HD) == 0
+            and PARTS * (feature // (CORES * HD)) <= HD
+        )
+        run = functools.partial(fast_body, n) if fits else body
+        return run(cache_kv, new_rows, cross_queries, enc_kv, lengths, parents)
+
     return jax.shard_map(
-        body, mesh=mesh, in_specs=placed, out_specs=P(("groups", "utt"), None), check_vma=False
-    )
+        either, mesh=mesh, in_specs=placed, out_specs=P(("groups", "utt"), None), check_vma=False
+    )

time: 56.2 us -> 35.9 us (0.64)
  Pallas kernels: 0 us -> 29.4 us
  waiting for transfers between devices: 22.7 us -> 0 us
  blocking collectives: 11.9 us -> 0 us
  starting transfers between devices: 11 us -> 0 us
  other arithmetic: 2.63 us -> 0 us
  matrix products: 1.41 us -> 0 us
    pallas_call x0 -> x1, Pallas kernels: none -> 29.4 us  [fast_body(): pl.pallas_call(functools.partial(fast_kernel, n), out_shape=jax.ShapeDtyp...]
    all_to_all x2 -> x0, waiting for transfers between devices: 22.7 us -> none  [the longest x1 17.2 us: body(): lax.all_to_all(cache_kv, 'utt', split_axis=0, concat_axis=0, tiled=True)]
    all_to_all x1 -> x0, blocking collectives: 11.9 us -> none  [body(): lax.all_to_all(mixed_here, 'utt', split_axis=0, concat_axis=0, tiled=True)]
    all_to_all x2 -> x0, starting transfers between devices: 11 us -> none  [the longest x1 7.41 us: body(): lax.all_to_all(new_rows, 'utt', split_axis=0, concat_axis=0, tiled=True)]
    unnamed x12 -> x11, local copies, waits for them, and re-layouts: 2.06 us -> 5.52 us
    all_to_all x1 -> x0, other arithmetic: 1.6 us -> none  [body(): lax.all_to_all(new_rows, 'utt', split_axis=0, concat_axis=0, tiled=True)]
    slice x1 -> x0, local copies, waits for them, and re-layouts: 1.47 us -> none  [attend_frames(): frames_kv[:, :, :feature].reshape(utterances, frame_total, head_count, HD)]
    dot_general x3 -> x0, matrix products: 1.03 us -> none  [the longest x1 0.35 us: attend_frames(): jnp.einsum('uhbf,ufhd->ubhd', weights, value_heads, preferred_element_typ...]
  transfers between devices with their start and end apart: 2 -> 0, of which waited for: 2 -> 0; matrix products, arithmetic and copies ran while one was open for 6% -> 0% of each run, Pallas kernels for 0% -> 0%
where the time goes in v1:
time: 35.9 us; the launch traced here: 35.6 us
  Pallas kernels  29.4 us (82%)
  local copies, waits for them, and re-layouts  5.52 us (15%)
  between operations  0.67 us (2%)
    pallas_call x1, Pallas kernels, fast_body(): pl.pallas_call(functools.partial(fast_kernel, n), out_shape=jax.ShapeDtyp...  29.4 us
    unnamed x11, local copies, waits for them, and re-layouts  5.52 us

profile of v1, /device:TPU:0, one launch (start us, length us, event | category | flops | bytes accessed | tf_op | source)
XLA Modules:
  0.0 35.6 jit_solution(808664426610958837)
XLA Ops:
  0.7 0.0 copy-start
  0.7 1.4 %copy-done = bf16[1,256,3072]{2,1,0:T(8,128)(2,1)S(1)} copy-done((bf16[1,256,3072]{2,1,0:T(8,128)(2,1)S(1)}, bf16[1,256,3072]{2,1,0:T(8,128)(2,1)}, u32[]{:S(2)}) %copy-start) | copy-done | bytes 1572888
  2.1 0.0 copy-start.1
  2.1 1.1 %copy-done.1 = bf16[16,8,3072]{2,1,0:T(8,128)(2,1)S(1)} copy-done((bf16[16,8,3072]{2,1,0:T(8,128)(2,1)S(1)}, bf16[16,8,3072]{2,1,0:T(8,128)(2,1)}, u32[]{:S(2)}) %copy-start.1) | copy-done | bytes 786456
  3.2 0.0 copy-start.2
  3.2 0.9 %copy-done.2 = bf16[16,4608]{1,0:T(8,128)(2,1)S(1)} copy-done((bf16[16,4608]{1,0:T(8,128)(2,1)S(1)}, bf16[16,4608]{1,0:T(8,128)(2,1)}, u32[]{:S(2)}) %copy-start.2) | copy-done | bytes 147480
  4.1 0.0 copy-start.3
  4.1 0.8 %copy-done.3 = bf16[16,1536]{1,0:T(8,128)(2,1)S(1)} copy-done((bf16[16,1536]{1,0:T(8,128)(2,1)S(1)}, bf16[16,1536]{1,0:T(8,128)(2,1)}, u32[]{:S(2)}) %copy-start.3) | copy-done | bytes 49176
  4.9 0.0 copy-start.4
  4.9 0.7 %copy-done.4 = s32[1,16]{1,0:T(1,128)S(1)} copy-done((s32[1,16]{1,0:T(1,128)S(1)}, s32[1,16]{1,0:T(1,128)}, u32[]{:S(2)}) %copy-start.4) | copy-done | bytes 88
  5.6 29.4 %shard_map.64 = bf16[16,1536]{1,0:T(8,128)(2,1)S(1)} custom-call(bf16[128,3072]{1,0:T(8,128)(2,1)S(1)} %bitcast.1, bf16[16,4608]{1,0:T(8,128)(2,1)S(1)} %copy-done.2, bf16[16,1536]{1,0:T(8,128)(2,1)S(1)} %copy-done.3, bf16[1,256,3072]{2,1,0:T(8,128)(2,1)S(1)} %copy-done, s32[1]{0:T(128)S(6)} %copy.8.len_ref, s32[1,16]{1,0:T(1,128)S(1)} %copy-done.4), custom_call_target="tpu_custom_call" | custom-call | tf_op jit(solution)/shard_map/pallas_call | solution.py:292
  35.0 0.6 %copy.9 = bf16[16,1536]{1,0:T(8,128)(2,1)} copy(bf16[16,1536]{1,0:T(8,128)(2,1)S(1)} %shard_map.64) | data formatting | bytes 98304
Async XLA Ops:
  0.7 1.4 %copy-start = (bf16[1,256,3072]{2,1,0:T(8,128)(2,1)S(1)}, bf16[1,256,3072]{2,1,0:T(8,128)(2,1)}, u32[]{:S(2)}) copy-start(bf16[1,256,3072]{2,1,0:T(8,128)(2,1)} %enc_ref.1) | copy-start | bytes 4718596
  2.1 1.1 %copy-start.1 = (bf16[16,8,3072]{2,1,0:T(8,128)(2,1)S(1)}, bf16[16,8,3072]{2,1,0:T(8,128)(2,1)}, u32[]{:S(2)}) copy-start(bf16[16,8,3072]{2,1,0:T(8,128)(2,1)} %param.6) | copy-start | bytes 2359300
  3.2 0.9 %copy-start.2 = (bf16[16,4608]{1,0:T(8,128)(2,1)S(1)}, bf16[16,4608]{1,0:T(8,128)(2,1)}, u32[]{:S(2)}) copy-start(bf16[16,4608]{1,0:T(8,128)(2,1)} %new_ref.1) | copy-start | bytes 442372
  4.1 0.8 %copy-start.3 = (bf16[16,1536]{1,0:T(8,128)(2,1)S(1)}, bf16[16,1536]{1,0:T(8,128)(2,1)}, u32[]{:S(2)}) copy-start(bf16[16,1536]{1,0:T(8,128)(2,1)} %cq_ref.1) | copy-start | bytes 147460
  4.9 0.7 %copy-start.4 = (s32[1,16]{1,0:T(1,128)S(1)}, s32[1,16]{1,0:T(1,128)}, u32[]{:S(2)}) copy-start(s32[1,16]{1,0:T(1,128)} %par_ref.1) | copy-start | bytes 196

commit v2 on v1

--- a/solution.py
+++ b/solution.py
@@ -78,7 +78,7 @@
 
     sends = []
     slot = 0
-    for dz in (2, 1, 3, 0):
+    for dz in (*range(1, depth), 0):
         zz = lax.rem(z + dz, depth)
         for dc in range(CORES):
             cc = lax.rem(c + dc, CORES)
@@ -137,7 +137,7 @@
 
     copies[3].wait()
     slot = 0
-    for dz in (1, 3, 2):
+    for dz in range(1, depth):
         zz = lax.rem(z + dz, depth)
         for cc in range(CORES):
             src = at(zz, y, cc)
@@ -208,7 +208,7 @@
 
     across = at(z, y_other, c)
     y_in = []
-    for dz in (2, 1, 3, 0):
+    for dz in (*range(1, depth), 0):
         zz = lax.rem(z + dz, depth)
         cp = remote(ctx.at[zz, y_other], ybuf.at[dz], y_send.at[dz], y_recv.at[dz], across)
         cp.start()
@@ -316,7 +316,7 @@
             dma((depth,)), dma((depth,)), dma((depth * CORES - 1,)), dma((depth * CORES,)),
         ],
         compiler_params=pltpu.CompilerParams(
-            collective_id=0, has_side_effects=True, vmem_limit_bytes=48 << 20
+            collective_id=0, has_side_effects=True, vmem_limit_bytes=67043328
         ),
     )(cache_kv.reshape(old, width), new_rows, cross_queries, enc_kv, lengths, parents)
 
@@ -428,7 +428,7 @@
         fits = (
             parents.shape == (1, n)
             and cache_kv.shape[0] == n
-            and n == 4 * CORES * LINES
+            and n % (CORES * LINES) == 0
             and feature % (CORES * HD) == 0
             and PARTS * (feature // (CORES * HD)) <= HD
         )

time: 35.9 us -> 32.7 us (0.911)
  local copies, waits for them, and re-layouts: 5.52 us -> 1.42 us
  Pallas kernels: 29.4 us -> 30.4 us
    unnamed x11 -> x1, local copies, waits for them, and re-layouts: 5.52 us -> 1.42 us
    pallas_call x1, Pallas kernels: 29.4 us -> 30.4 us  [fast_body(): pl.pallas_call(functools.partial(fast_kernel, n), out_shape=jax.ShapeDtyp...]
where the time goes in v2:
time: 32.7 us; the launch traced here: 32.5 us
  Pallas kernels  30.4 us (93%)
  local copies, waits for them, and re-layouts  1.42 us (4%)
  between operations  0.66 us (2%)
    pallas_call x1, Pallas kernels, fast_body(): pl.pallas_call(functools.partial(fast_kernel, n), out_shape=jax.ShapeDtyp...  30.4 us
    unnamed x1, local copies, waits for them, and re-layouts  1.42 us

profile of v2, /device:TPU:0, one launch (start us, length us, event | category | flops | bytes accessed | tf_op | source)
XLA Modules:
  0.0 32.5 jit_solution(17082320084142437637)
XLA Ops:
  0.7 30.4 %shard_map.64 = bf16[16,1536]{1,0:T(8,128)(2,1)} custom-call(bf16[128,3072]{1,0:T(8,128)(2,1)} %bitcast.1, bf16[16,4608]{1,0:T(8,128)(2,1)} %new_ref.1, bf16[16,1536]{1,0:T(8,128)(2,1)} %cq_ref.1, bf16[1,256,3072]{2,1,0:T(8,128)(2,1)} %enc_ref.1, s32[1]{0:T(128)S(6)} %copy.8.len_ref, s32[1,16]{1,0:T(1,128)} %par_ref.1), custom_call_target="tpu_custom_call" | custom-call | tf_op jit(solution)/shard_map/pallas_call | solution.py:292
  31.1 1.4 %copy.9 = bf16[16,1536]{1,0:T(8,128)(2,1)} copy(bf16[16,1536]{1,0:T(8,128)(2,1)} %shard_map.64) | data formatting | bytes 98304

commit v3 on v2

--- a/solution.py
+++ b/solution.py
@@ -11,6 +11,7 @@
 CORES = 2
 LINES = 2
 PARTS = 3
+CHUNKS = 2
 LOW = -1e30
 
 
@@ -24,11 +25,14 @@
     out_ref,
     qbuf, kbuf, vbuf, newbuf, cqbuf, encbuf, ptab, ctx, ybuf, sbuf, zbuf, xsend, xrecv,
     local_sem, q_send, q_recv, f_send, c_send, c_recv, p_send, p_recv, x_send, x_recv,
-    y_send, y_recv, z_send, z_recv,
+    y_send, y_recv, z_send, z_recv, qown_sem, stay_sem,
 ):
     feature = cq_ref.shape[1]
     half = feature // CORES
     heads = half // HD
+    chunks = CHUNKS if heads % CHUNKS == 0 else 1
+    chunk_heads = heads // chunks
+    width = chunk_heads * HD
     rows = cq_ref.shape[0]
     utts = new_ref.shape[0]
     old = cache_ref.shape[0]
@@ -58,6 +62,9 @@
             barrier, inc=1, device_id={"utt": lax.rem(me + k, n)},
             device_id_type=pl.DeviceIdType.MESH,
         )
+
+    def chunk_cols(cc, k):
+        return pl.ds(pl.multiple_of(cc * half + k * width, HD), width)
 
     my_half = pl.ds(pl.multiple_of(c * half, HD), half)
     my_values = pl.ds(pl.multiple_of(feature + c * half, HD), half)
@@ -66,45 +73,15 @@
         pltpu.make_async_copy(cq_ref, cqbuf, local_sem.at[0]),
         pltpu.make_async_copy(enc_ref.at[0], encbuf, local_sem.at[1]),
         pltpu.make_async_copy(new_ref, newbuf, local_sem.at[2]),
-        pltpu.make_async_copy(new_ref.at[:, my_half], qbuf.at[z, y, c], local_sem.at[3]),
         pltpu.make_async_copy(cache_ref.at[:, my_half], kbuf.at[my_rows], local_sem.at[4]),
         pltpu.make_async_copy(cache_ref.at[:, my_values], vbuf.at[my_rows], local_sem.at[5]),
         pltpu.make_async_copy(par_ref, ptab.at[me], local_sem.at[6]),
+    ] + [
+        pltpu.make_async_copy(new_ref.at[:, chunk_cols(c, k)], qbuf.at[k, z, y, c], qown_sem.at[k])
+        for k in range(chunks)
     ]
     for cp in copies:
         cp.start()
-
-    pl.semaphore_wait(barrier, n - 1)
-
-    sends = []
-    slot = 0
-    for dz in (*range(1, depth), 0):
-        zz = lax.rem(z + dz, depth)
-        for dc in range(CORES):
-            cc = lax.rem(c + dc, CORES)
-            cols = pl.ds(pl.multiple_of(cc * half, HD), half)
-            for yy in (y, y_other) if dz == 0 else (y,):
-                if dz == 0 and dc == 0 and yy is y:
-                    continue
-                cp = remote(new_ref.at[:, cols], qbuf.at[z, y, c], q_send.at[slot],
-                            q_recv.at[me], at(zz, yy, cc))
-                cp.start()
-                sends.append(cp)
-                slot += 1
-    for k in range(1, n):
-        dev = lax.rem(me + k, n)
-        cp = remote(par_ref, ptab.at[me], p_send.at[k - 1], p_recv.at[me], dev)
-        cp.start()
-        sends.append(cp)
-    other_half = pl.ds(pl.multiple_of(c_other * half, HD), half)
-    other_values = pl.ds(pl.multiple_of(feature + c_other * half, HD), half)
-    partner = at(z, y, c_other)
-    cache_in = []
-    for i, (cols, buf) in enumerate(((other_half, kbuf), (other_values, vbuf))):
-        cp = remote(cache_ref.at[:, cols], buf.at[my_rows], c_send.at[i], c_recv.at[i], partner)
-        cp.start()
-        sends.append(cp)
-        cache_in.append(cp)
 
     copies[0].wait()
     copies[1].wait()
@@ -124,7 +101,64 @@
         for b in range(rows):
             xsend[b, :, cols] = o[b : b + 1, :]
 
-    for h in range(feature // HD):
+    early = (feature // HD) // 3
+    for h in range(early):
+        cross(h)
+
+    copies[2].wait()
+    pl.semaphore_wait(barrier, n - 1)
+
+    sends = []
+
+    def spread(k):
+        slot = 0
+        for dz in (*range(1, depth), 0):
+            zz = lax.rem(z + dz, depth)
+            for dc in range(CORES):
+                cc = lax.rem(c + dc, CORES)
+                for yy in (y_other, y) if dz == 0 else (y,):
+                    if dz == 0 and dc == 0 and yy is y:
+                        continue
+                    cp = remote(newbuf.at[:, chunk_cols(cc, k)], qbuf.at[k, z, y, c],
+                                q_send.at[k, slot], q_recv.at[k, me], at(zz, yy, cc))
+                    cp.start()
+                    sends.append(cp)
+                    slot += 1
+
+    spread(0)
+    for k in range(1, n):
+        dev = lax.rem(me + k, n)
+        cp = remote(par_ref, ptab.at[me], p_send.at[k - 1], p_recv.at[me], dev)
+        cp.start()
+        sends.append(cp)
+    for k in range(1, chunks):
+        spread(k)
+    other_half = pl.ds(pl.multiple_of(c_other * half, HD), half)
+    other_values = pl.ds(pl.multiple_of(feature + c_other * half, HD), half)
+    partner = at(z, y, c_other)
+    cache_in = []
+    for i, (cols, buf) in enumerate(((other_half, kbuf), (other_values, vbuf))):
+        cp = remote(cache_ref.at[:, cols], buf.at[my_rows], c_send.at[i], c_recv.at[i], partner)
+        cp.start()
+        sends.append(cp)
+        cache_in.append(cp)
+
+    def forward(k):
+        slot = 0
+        for dz in range(1, depth):
+            zz = lax.rem(z + dz, depth)
+            for cc in range(CORES):
+                src = at(zz, y, cc)
+                piece = qbuf.at[k, zz, y, cc]
+                remote(piece, piece, f_send.at[k, slot], q_recv.at[k, src], src).wait_recv()
+                cp = remote(piece, piece, f_send.at[k, slot], q_recv.at[k, src], at(z, y_other, c))
+                cp.start()
+                sends.append(cp)
+                slot += 1
+
+    forward(0)
+
+    for h in range(early, feature // HD):
         cross(h)
 
     own_x = pltpu.make_async_copy(xsend.at[me], xrecv.at[me], local_sem.at[7])
@@ -136,25 +170,10 @@
         sends.append(cp)
 
     copies[3].wait()
-    slot = 0
-    for dz in range(1, depth):
-        zz = lax.rem(z + dz, depth)
-        for cc in range(CORES):
-            src = at(zz, y, cc)
-            piece = qbuf.at[zz, y, cc]
-            remote(piece, piece, f_send.at[slot], q_recv.at[src], src).wait_recv()
-            cp = remote(piece, piece, f_send.at[slot], q_recv.at[src], at(z, y_other, c))
-            cp.start()
-            sends.append(cp)
-            slot += 1
-    piece = qbuf.at[z, y, c_other]
-    remote(piece, piece, f_send.at[0], q_recv.at[partner], partner).wait_recv()
-
     copies[4].wait()
-    copies[5].wait()
     for cp in cache_in:
         cp.wait_recv()
-    copies[6].wait()
+    copies[5].wait()
     for k in range(1, n):
         src = lax.rem(me + n - k, n)
         remote(par_ref, ptab.at[src], p_send.at[0], p_recv.at[src], src).wait_recv()
@@ -166,97 +185,128 @@
     keys = CORES * old
     ones_k = jnp.ones((keys, HD), jnp.bfloat16)
 
-    def partial(yy):
+    def masks(yy):
         target = []
         for zz in range(depth):
             for cc in range(CORES):
                 col = jnp.sum(jnp.where(beam_lane == at(zz, yy, cc), table, 0), axis=1, keepdims=True)
                 target.append((col - chip * CORES) * utts + row_u)
         target = jnp.concatenate(target, axis=0)
-        count = depth * CORES * utts
         valid = lax.broadcasted_iota(jnp.int32, (count, keys), 1) // history == target
         sel = jnp.broadcast_to((target >= 0) & (target < CORES * utts), (count, HD))
-        lane = lax.broadcasted_iota(jnp.int32, (count, HD), 1)
-        stats = jnp.zeros((count, HD), jnp.float32)
-        for h in range(heads):
+        return valid, sel
+
+    count = depth * CORES * utts
+    lane = lax.broadcasted_iota(jnp.int32, (count, HD), 1)
+
+    def partial(yy, mask, stats, k):
+        valid, sel = mask
+        for hk in range(chunk_heads):
+            h = k * chunk_heads + hk
             cols = slice(h * HD, (h + 1) * HD)
-            q = qbuf[:, pl.ds(yy, 1), :, :, cols].reshape(count, HD)
+            kcols = slice(hk * HD, (hk + 1) * HD)
+            q = qbuf[k, :, pl.ds(yy, 1), :, :, kcols].reshape(count, HD)
             s = jnp.where(valid, contract_last(q, kbuf[:, cols]) * scale, LOW)
             m = jnp.max(s, axis=1, keepdims=True)
             p = jnp.where(valid, jnp.exp(s - m), 0.0).astype(jnp.bfloat16)
             v = jnp.concatenate([vbuf[:, cols], ones_k], axis=1)
             o = jnp.dot(p, v, preferred_element_type=jnp.float32)
             total = jnp.where(sel, o[:, HD:], 1.0)
-            ctx[:, pl.ds(yy, 1), :, :, cols] = (o[:, :HD] / total).astype(jnp.bfloat16).reshape(
+            ctx[k][:, pl.ds(yy, 1), :, :, kcols] = (o[:, :HD] / total).astype(jnp.bfloat16).reshape(
                 depth, 1, CORES, utts, HD)
             rest = jnp.where(sel, m + jnp.log(total), 0.0)
-            for k in range(PARTS):
+            for j in range(PARTS):
                 part = rest.astype(jnp.bfloat16).astype(jnp.float32)
-                stats = jnp.where(lane == PARTS * h + k, part, stats)
+                stats = jnp.where(lane == PARTS * h + j, part, stats)
                 rest = rest - part
-        ctx[:, pl.ds(yy, 1), :, :, half:] = stats.astype(jnp.bfloat16).reshape(
-            depth, 1, CORES, utts, HD)
-
-    partial(y)
-
-    for zz in range(depth):
-        for cc in range(CORES):
-            src = at(zz, y_other, cc)
-            piece = qbuf.at[zz, y_other, cc]
-            remote(piece, piece, f_send.at[0], q_recv.at[src], src).wait_recv()
-    partial(y_other)
+        if k == chunks - 1:
+            ctx[k][:, pl.ds(yy, 1), :, :, width:] = stats.astype(jnp.bfloat16).reshape(
+                depth, 1, CORES, utts, HD)
+        return stats
 
     across = at(z, y_other, c)
-    y_in = []
-    for dz in (*range(1, depth), 0):
-        zz = lax.rem(z + dz, depth)
-        cp = remote(ctx.at[zz, y_other], ybuf.at[dz], y_send.at[dz], y_recv.at[dz], across)
-        cp.start()
-        sends.append(cp)
-        y_in.append((dz, zz, cp))
-
-    copies[2].wait()
+    y_in = [[] for _ in range(chunks)]
+
+    def turn(k):
+        for dz in (*range(1, depth), 0):
+            zz = lax.rem(z + dz, depth)
+            cp = remote(ctx[k].at[zz, y_other], ybuf[k].at[dz], y_send.at[k, dz], y_recv.at[k, dz],
+                        across)
+            cp.start()
+            sends.append(cp)
+            y_in[k].append((dz, zz, cp))
+
+    stays = []
+
+    def deliver(k):
+        slot = 0
+        for dz, zz, cp in y_in[k]:
+            cp.wait_recv()
+            sbuf[k][dz] = ctx[k][pl.ds(zz, 1), pl.ds(y, 1)].reshape(sbuf[k].shape[1:]) + ybuf[k][dz]
+            for dc in range(CORES):
+                cc = lax.rem(c + dc, CORES)
+                if dz == 0 and dc == 0:
+                    stay = pltpu.make_async_copy(sbuf[k].at[dz, cc], zbuf[k].at[z, c], stay_sem.at[k])
+                    stay.start()
+                    stays.append(stay)
+                    continue
+                cp = remote(sbuf[k].at[dz, cc], zbuf[k].at[z, c], z_send.at[k, slot],
+                            z_recv.at[k, z * CORES + c], at(zz, y, cc))
+                cp.start()
+                sends.append(cp)
+                slot += 1
+
+    mask_here, mask_there = masks(y), masks(y_other)
+    stats_here = stats_there = jnp.zeros((count, HD), jnp.float32)
+    for k in range(chunks):
+        piece = qbuf.at[k, z, y, c_other]
+        remote(piece, piece, f_send.at[k, 0], q_recv.at[k, partner], partner).wait_recv()
+        copies[6 + k].wait()
+        if k + 1 < chunks:
+            forward(k + 1)
+        stats_here = partial(y, mask_here, stats_here, k)
+        for zz in range(depth):
+            for cc in range(CORES):
+                src = at(zz, y_other, cc)
+                piece = qbuf.at[k, zz, y_other, cc]
+                remote(piece, piece, f_send.at[k, 0], q_recv.at[k, src], src).wait_recv()
+        stats_there = partial(y_other, mask_there, stats_there, k)
+        turn(k)
+        if k > 0:
+            deliver(k - 1)
+
     own = []
     for h in range(feature // HD):
         q = newbuf[:, h * HD : (h + 1) * HD].astype(jnp.float32)
         k = newbuf[:, feature + h * HD : feature + (h + 1) * HD].astype(jnp.float32)
         own.append(jnp.sum(q * k, axis=1, keepdims=True) * scale)
 
-    slot = 0
-    for dz, zz, cp in y_in:
-        cp.wait_recv()
-        sbuf[dz] = (ctx[pl.ds(zz, 1), pl.ds(y, 1)].reshape(CORES, utts, half + HD) + ybuf[dz])
-        for dc in range(CORES):
-            cc = lax.rem(c + dc, CORES)
-            if dz == 0 and dc == 0:
-                stay = pltpu.make_async_copy(sbuf.at[dz, cc], zbuf.at[z, c], local_sem.at[8])
-                stay.start()
-                continue
-            cp = remote(sbuf.at[dz, cc], zbuf.at[z, c], z_send.at[slot], z_recv.at[z * CORES + c],
-                        at(zz, y, cc))
-            cp.start()
-            sends.append(cp)
-            slot += 1
+    deliver(chunks - 1)
 
     own_x.wait()
     for k in range(1, n):
         src = lax.rem(me + n - k, n)
         remote(xsend.at[src], xrecv.at[src], x_send.at[0], x_recv.at[src], src).wait_recv()
 
-    stay.wait()
-    for dz in range(depth):
-        zz = lax.rem(z + dz, depth)
-        for dc in range(CORES):
-            if dz == 0 and dc == 0:
-                continue
-            cc = lax.rem(c + dc, CORES)
-            remote(zbuf.at[zz, cc], zbuf.at[zz, cc], z_send.at[0], z_recv.at[zz * CORES + cc],
-                   at(zz, y, cc)).wait_recv()
+    for stay in stays:
+        stay.wait()
+    for k in range(chunks):
+        for dz in range(depth):
+            zz = lax.rem(z + dz, depth)
+            for dc in range(CORES):
+                if dz == 0 and dc == 0:
+                    continue
+                cc = lax.rem(c + dc, CORES)
+                remote(zbuf[k].at[zz, cc], zbuf[k].at[zz, cc], z_send.at[k, 0],
+                       z_recv.at[k, zz * CORES + cc], at(zz, y, cc)).wait_recv()
 
     for cc in range(CORES):
-        both = zbuf[0, cc].astype(jnp.float32)
-        for zz in range(1, depth):
-            both = both + zbuf[zz, cc].astype(jnp.float32)
+        both = []
+        for k in range(chunks):
+            both.append(zbuf[k][0, cc].astype(jnp.float32))
+            for zz in range(1, depth):
+                both[k] = both[k] + zbuf[k][zz, cc].astype(jnp.float32)
+        both = jnp.concatenate(both, axis=1)
         stats = both[:, half:]
         lane = lax.broadcasted_iota(jnp.int32, stats.shape, 1)
         for hl in range(heads):
@@ -285,6 +335,10 @@
     half = feature // CORES
     old = utts * history
     depth = n // (CORES * LINES)
+    heads = half // HD
+    chunks = CHUNKS if heads % CHUNKS == 0 else 1
+    w = half // chunks
+    wide = [w] * (chunks - 1) + [w + HD]
     frames = enc_kv.shape[1]
     bf = jnp.bfloat16
     dma = pltpu.SemaphoreType.DMA
@@ -296,24 +350,25 @@
                   pl.BlockSpec(memory_space=pltpu.VMEM)],
         out_specs=pl.BlockSpec(memory_space=pltpu.VMEM),
         scratch_shapes=[
-            pltpu.VMEM((depth, LINES, CORES, utts, half), bf),
+            pltpu.VMEM((chunks, depth, LINES, CORES, utts, w), bf),
             pltpu.VMEM((CORES * old, half), bf),
             pltpu.VMEM((CORES * old, half), bf),
             pltpu.VMEM(new_rows.shape, bf),
             pltpu.VMEM(cross_queries.shape, bf),
             pltpu.VMEM((frames, width), bf),
             pltpu.VMEM((n,) + parents.shape, jnp.int32),
-            pltpu.VMEM((depth, LINES, CORES, utts, half + HD), bf),
-            pltpu.VMEM((depth, CORES, utts, half + HD), bf),
-            pltpu.VMEM((depth, CORES, utts, half + HD), bf),
-            pltpu.VMEM((depth, CORES, utts, half + HD), bf),
+            [pltpu.VMEM((depth, LINES, CORES, utts, v), bf) for v in wide],
+            [pltpu.VMEM((depth, CORES, utts, v), bf) for v in wide],
+            [pltpu.VMEM((depth, CORES, utts, v), bf) for v in wide],
+            [pltpu.VMEM((depth, CORES, utts, v), bf) for v in wide],
             pltpu.VMEM((rows, 1, feature), jnp.float32),
             pltpu.VMEM((utts, 1, feature), jnp.float32),
-            dma((9,)),
-            dma((depth * CORES + 1,)), dma((n,)), dma(((depth - 1) * CORES,)),
+            dma((8,)),
+            dma((chunks, depth * CORES + 1)), dma((chunks, n)), dma((chunks, (depth - 1) * CORES)),
             dma((2,)), dma((2,)),
             dma((n - 1,)), dma((n,)), dma((n - 1,)), dma((n,)),
-            dma((depth,)), dma((depth,)), dma((depth * CORES - 1,)), dma((depth * CORES,)),
+            dma((chunks, depth)), dma((chunks, depth)),
+            dma((chunks, depth * CORES - 1)), dma((chunks, depth * CORES)), dma((chunks,)), dma((chunks,)),
         ],
         compiler_params=pltpu.CompilerParams(
             collective_id=0, has_side_effects=True, vmem_limit_bytes=67043328

time: 32.7 us -> 30.4 us (0.930)
  Pallas kernels: 30.4 us -> 28.1 us
    pallas_call x1, Pallas kernels: 30.4 us -> 28.1 us  [fast_body(): pl.pallas_call(functools.partial(fast_kernel, n), out_shape=jax.ShapeDtyp...]
where the time goes in v3:
time: 30.4 us; the launch traced here: 30.2 us
  Pallas kernels  28.1 us (92%)
  local copies, waits for them, and re-layouts  1.42 us (5%)
  between operations  0.66 us (2%)
    pallas_call x1, Pallas kernels, fast_body(): pl.pallas_call(functools.partial(fast_kernel, n), out_shape=jax.ShapeDtyp...  28.1 us
    unnamed x1, local copies, waits for them, and re-layouts  1.42 us

profile of v3, /device:TPU:0, one launch (start us, length us, event | category | flops | bytes accessed | tf_op | source)
XLA Modules:
  0.0 30.2 jit_solution(4511293031881455674)
XLA Ops:
  0.7 28.1 %shard_map.64 = bf16[16,1536]{1,0:T(8,128)(2,1)} custom-call(bf16[128,3072]{1,0:T(8,128)(2,1)} %bitcast.1, bf16[16,4608]{1,0:T(8,128)(2,1)} %new_ref.1, bf16[16,1536]{1,0:T(8,128)(2,1)} %cq_ref.1, bf16[1,256,3072]{2,1,0:T(8,128)(2,1)} %enc_ref.1, s32[1]{0:T(128)S(6)} %copy.8.len_ref, s32[1,16]{1,0:T(1,128)} %par_ref.1), custom_call_target="tpu_custom_call" | custom-call | tf_op jit(solution)/shard_map/pallas_call | solution.py:346
  28.7 1.4 %copy.9 = bf16[16,1536]{1,0:T(8,128)(2,1)} copy(bf16[16,1536]{1,0:T(8,128)(2,1)} %shard_map.64) | data formatting | bytes 98304
